TPU v7x, 32 devices: a whole 2x2x4 slice. The times are simulated.
32 devices in a mesh: cone: 4 (over y, x), con: 8 (over z, core).
Axes of the slice: x: 2, y: 2, z: 4, core: 2. Of those that a mesh axis runs over, the one named last changes fastest.
Arguments:
- vectors: bfloat16 [4, 8192, 1024], P('cone', 'con'), may hold values from -0.1875 to 0.1875
- primal: bfloat16 [4, 1024, 1024], P('cone'), may hold values from -8 to 8, as said below
- dual_inverse: bfloat16 [4, 1024, 1024], P('cone'), may hold values from -8 to 8, as said below
- touches: int32 [4, 8], P('cone'), may hold values from 0 to 1, as said below
Outputs:
- slab: float32 [2048, 8192], P('cone', 'con')
Inputs may be any that keep to these rules, and one draw needn't show every extreme that they name: `primal`: symmetric and positive definite in every cone. `dual_inverse`: symmetric and positive definite in every cone. Every constraint block touches at least one cone.
All inputs are finite; a program needn't handle non-finite values.
Results may differ from a plain program's by a relative error of at most 0.00079.
Values may be sent and summed in bfloat16 or wider, within the bound.
No kernel may reach another device: no remote copies, remote signals or barrier semaphores. Data moves between devices by JAX's collectives and lax.ppermute only.
A program may use at most 128 MiB of HBM per device.

v0:
```python
import jax
import jax.numpy as jnp
from jax import lax
from jax.sharding import PartitionSpec as P

PANEL = 512


def broadcast(value, axis, source):
    kept = jnp.where(lax.axis_index(axis) == source, value, 0).astype(value.dtype)
    return lax.psum(kept, axis)


def shards(vectors, primal, dual_inverse, touches):
    con_count = lax.axis_size("con")
    cone_count = lax.axis_size("cone")
    con_place = lax.axis_index("con")
    cone_place = lax.axis_index("cone")
    per_block = vectors.shape[1]
    row_dev = PANEL * cone_count // con_count
    owners = con_count // cone_count
    touched = touches[0]
    own_flag = lax.dynamic_index_in_dim(touched, con_place, 0, keepdims=False)
    own_vectors = vectors[0] * own_flag.astype(jnp.bfloat16)
    primal_block = primal[0]
    dual_block = dual_inverse[0]
    row_vectors = lax.all_gather(own_vectors[:row_dev], "con", axis=0, tiled=True)
    row_primal = jnp.dot(row_vectors, primal_block, preferred_element_type=jnp.float32).astype(
        jnp.bfloat16
    )
    row_dual = jnp.dot(row_vectors, dual_block, preferred_element_type=jnp.float32).astype(
        jnp.bfloat16
    )
    contract = (((1,), (1,)), ((), ()))
    gram_primal = lax.dot_general(
        row_primal, own_vectors, contract, preferred_element_type=jnp.float32
    )
    gram_dual = lax.dot_general(row_dual, own_vectors, contract, preferred_element_type=jnp.float32)
    schur_slab = lax.psum_scatter(gram_primal * gram_dual, "cone", scatter_dimension=0, tiled=True)
    panel_block = broadcast(schur_slab, "cone", 0)
    leading_columns = panel_block[:, :row_dev]
    gathered = lax.all_gather(leading_columns, "con", axis=1, tiled=True)
    pivot_source = gathered[:, :PANEL]
    block_source = lax.dynamic_slice_in_dim(gathered, cone_place * PANEL, PANEL, 1)
    pivot_matrix = (pivot_source + pivot_source.T) * 0.5
    lower_factor = jnp.linalg.cholesky(pivot_matrix)
    combined = jnp.concatenate([panel_block, block_source], axis=1)
    solved = jax.scipy.linalg.solve_triangular(lower_factor, combined, lower=True)
    factor_rows = solved[:, :per_block]
    row_factor = solved[:, per_block:]
    updated = schur_slab - jnp.einsum(
        "kr,kc->rc", row_factor, factor_rows, precision=lax.Precision.HIGHEST
    )
    local_columns = jnp.arange(per_block, dtype=jnp.int32)
    pivot_column = (con_place < owners) & (local_columns < row_dev)
    remaining = jnp.where(pivot_column[None, :], 0.0, updated)
    return jnp.where(cone_place == 0, factor_rows, remaining)


def solution(mesh):
    in_specs = (
        P("cone", "con", None),
        P("cone", None, None),
        P("cone", None, None),
        P("cone", None),
    )
    out_specs = P("cone", "con")
    return jax.shard_map(shards, mesh=mesh, in_specs=in_specs, out_specs=out_specs, check_vma=False)
```

profile of v0, /device:TPU:0, one launch (start us, length us, event | category | flops | bytes accessed | tf_op | source)
XLA Modules:
  0.0 488.2 jit_solution(6037763311798876884)
XLA Ops:
  6.5 1.4 fusion.61
  7.9 2.4 broadcast_multiply_fusion
  10.3 1.3 copy-done.7
  12.5 49.7 %all-gather.6.cloned.1.call-done = bf16[1,2048,1024]{2,1,0:T(8,128)(2,1)} async-done(((bf16[1,256,1024]{2,1,0:T(8,128)(2,1)}), bf16[1,2048,1024]{2,1,0:T(8,128)(2,1)}) %all-gather.6.cloned.1.call-update) | async-done | bytes 4194320 | tf_op jit(solution)/shard_map/all_gather | solution.py:27
  62.2 7.1 %fusion.2 = bf16[2048,1024]{1,0:T(8,128)(2,1)S(1)} fusion(bf16[1,2048,1024]{2,1,0:T(8,128)(2,1)} %all-gather.6.cloned.1.call-done, bf16[1,1024,1024]{2,1,0:T(8,128)(2,1)S(1)} %copy-done), kind=kOutput, calls=%fused_computation.8 | convolution fusion | flops 4294967296 | bytes 10485760 | tf_op jit(solution)/shard_map/dot_general | solution.py:28
  69.3 4.6 fusion.5
  73.9 4.7 fusion
  78.7 6.8 %convolution_multiply_fusion = f32[2048,1024]{0,1:T(8,128)} fusion(f32[2048,1024]{0,1:T(8,128)S(1)} %fusion.5, bf16[2048,1024]{1,0:T(8,128)(2,1)S(1)} %fusion, bf16[1,1024,1024]{2,1,0:T(8,128)(2,1)S(1)} %copy-done.8), kind=kOutput, calls=%fused_computation.5 | convolution fusion | flops 4297064448 | bytes 23068672 | tf_op jit(solution)/shard_map/dot_general | solution.py:38
  85.5 85.2 %reduce-scatter.2.cloned.1.call-done = f32[512,1024]{0,1:T(8,128)} async-done(((f32[2048,1024]{0,1:T(8,128)}), f32[512,1024]{0,1:T(8,128)}) %reduce-scatter.2.cloned.1.call-update) | async-done | bytes 2097168 | tf_op jit(solution)/shard_map/reduce_scatter | solution.py:39
  170.7 3.1 broadcast_select_fusion
  174.1 69.2 %all-reduce.3.cloned.1.call-done = f32[512,1024]{0,1:T(8,128)} async-done(((f32[512,1024]{0,1:T(8,128)}), f32[512,1024]{0,1:T(8,128)}) %all-reduce.3.cloned.1.call-update) | async-done | bytes 2097168 | tf_op jit(solution)/shard_map/psum | solution.py:11
  243.3 1.9 slice.150
  245.3 47.0 %all-gather.4.cloned.1.call-done = f32[512,2048]{0,1:T(8,128)} async-done(((f32[512,256]{0,1:T(8,128)}), f32[512,2048]{0,1:T(8,128)}) %all-gather.4.cloned.1.call-update) | async-done | bytes 4194320 | tf_op jit(solution)/shard_map/all_gather | solution.py:42
  292.3 1.7 fusion.60
  294.3 1.4 fusion.31
  296.4 1.0 copy-done.9
  297.4 11.7 %cholesky.104 = f32[128,128]{1,0:T(8,128)S(1)} custom-call(f32[128,128]{1,0:T(8,128)S(1)} %cholesky.266), custom_call_target="Cholesky" | custom-call | tf_op jit(solution)/shard_map/jit(cholesky)/cholesky | solution.py:46
  309.1 1.1 cholesky.224
  310.2 9.8 %custom-call.31 = f32[1,128,128]{1,2,0:T(8,128)S(1)} custom-call(f32[1,128,128]{2,1,0:T(8,128)S(1)} %get-tuple-element.34), custom_call_target="InvertDiagBlocksLowerTriangular" | custom-call | tf_op jit(solution)/shard_map/jit(cholesky)/cholesky | solution.py:46
  320.0 1.9 constant_dynamic-update-slice_fusion.3
  321.9 1.2 convolution_subtract_fusion.3
  323.2 11.7 %cholesky.217 = f32[128,128]{1,0:T(8,128)S(1)} custom-call(f32[128,128]{1,0:T(8,128)S(1)} %cholesky.270), custom_call_target="Cholesky" | custom-call | tf_op jit(solution)/shard_map/jit(cholesky)/cholesky | solution.py:46
  335.6 10.2 %custom-call.32 = f32[1,128,128]{1,2,0:T(8,128)S(1)} custom-call(f32[1,128,128]{2,1,0:T(8,128)S(1)} %get-tuple-element.31), custom_call_target="InvertDiagBlocksLowerTriangular" | custom-call | tf_op jit(solution)/shard_map/jit(cholesky)/cholesky | solution.py:46
  345.8 0.9 convolution_dynamic-update-slice_fusion
  346.7 1.6 convolution_subtract_fusion.4
  348.3 11.7 %cholesky.238 = f32[128,128]{1,0:T(8,128)S(1)} custom-call(f32[128,128]{1,0:T(8,128)S(1)} %cholesky.275), custom_call_target="Cholesky" | custom-call | tf_op jit(solution)/shard_map/jit(cholesky)/cholesky | solution.py:46
  361.3 9.8 %custom-call.33 = f32[1,128,128]{1,2,0:T(8,128)S(1)} custom-call(f32[1,128,128]{2,1,0:T(8,128)S(1)} %get-tuple-element.28), custom_call_target="InvertDiagBlocksLowerTriangular" | custom-call | tf_op jit(solution)/shard_map/jit(cholesky)/cholesky | solution.py:46
  372.0 1.4 convolution_subtract_fusion.5
  373.4 11.9 %cholesky.255 = f32[128,128]{1,0:T(8,128)S(1)} custom-call(f32[128,128]{1,0:T(8,128)S(1)} %convolution_subtract_fusion.5), custom_call_target="Cholesky" | custom-call | tf_op jit(solution)/shard_map/jit(cholesky)/cholesky | solution.py:46
  389.8 2.3 select_select_fusion.1
  392.1 14.0 %while.1 = (s32[]{:T(128)}, f32[512,512]{1,0:T(8,128)}, s32[4,2]{0,1:T(2,128)S(1)}, f32[4,128,128]{2,1,0:T(8,128)}, s32[]{:T(128)}) while((s32[]{:T(128)}, f32[512,512]{1,0:T(8,128)}, s32[4,2]{0,1:T(2,128)S(1)}, f32[4,128,128]{2,1,0:T(8,128)}, s32[]{:T(128)}) %tuple.28), condition=%wide.while_cond, body=%wide.while_body.sunk | while | flops 2 | bytes 132705 | solution.py:48
  392.7 2.9 bitcast_dynamic-update-slice_fusion.2
  396.3 2.9 bitcast_dynamic-update-slice_fusion.2
  399.8 2.9 bitcast_dynamic-update-slice_fusion.2
  403.3 2.8 bitcast_dynamic-update-slice_fusion.2
  406.1 40.1 %custom-call.34 = f32[4,128,128]{1,2,0:T(8,128)S(1)} custom-call(f32[4,128,128]{2,1,0:T(8,128)} %get-tuple-element.12), custom_call_target="InvertDiagBlocksLowerTriangular" | custom-call | tf_op jit(solution)/shard_map/jit(_solve_triangular)/triangular_solve | solution.py:48
  446.3 1.8 fusion.34
  448.0 2.3 copy.9
  450.3 2.6 convolution_subtract_fusion.2
  452.9 1.7 fusion.48
  454.7 2.3 copy.10
  456.9 4.1 convolution_subtract_fusion
  461.0 1.8 fusion.46
  462.8 2.3 copy.11
  465.1 6.1 %convolution_subtract_fusion.1 = f32[128,1536]{0,1:T(8,128)S(1)} fusion(f32[128,1536]{1,0:T(8,128)} %fusion.46, f32[128,1536]{1,0:T(8,128)} %fusion.48, f32[128,1536]{1,0:T(8,128)} %fusion.34, f32[512,512]{0,1:T(8,128)S(1)} %get-tuple-element.24, f32[512,1024]{0,1:T(8,128)S(1)} %copy-done.2, f32[512,512]{1,0:T(8,128)} %get-tuple-element.93), kind=kOutput, calls=%fused_computation.18 | convolution fusion | flops 907542528 | bytes 6488064 | tf_op jit(solution)/shard_map/jit(_solve_triangular)/triangular_solve | solution.py:48
  472.2 1.4 copy-done.3
  473.6 5.0 %select_select_fusion = f32[512,1024]{0,1:T(8,128)} fusion(f32[512,1024]{0,1:T(8,128)S(1)} %copy-done.3, f32[512,1536]{0,1:T(8,128)S(1)} %pad_maximum_fusion, f32[128,1536]{0,1:T(8,128)S(1)} %fusion.45, f32[128,1536]{0,1:T(8,128)S(1)} %copy-done.6, f32[128,1536]{0,1:T(8,128)S(1)} %copy-done.5, f32[128,1536]{0,1:T(8,128)S(1)} %copy-done.4, ...), kind=kOutput, calls=%fused_computation.29 | convolution fusion | flops 3223584768 | bytes 11535361 | tf_op jit(solution)/shard_map/kr,kc->rc/dot_general | solution.py:51
  478.6 2.9 copy.14
  (58 shorter events, 10.6 us)
Async XLA Ops:
  6.5 55.7 %copy-start = (bf16[1,1024,1024]{2,1,0:T(8,128)(2,1)S(1)}, bf16[1,1024,1024]{2,1,0:T(8,128)(2,1)}, u32[]{:S(2)}) copy-start(bf16[1,1024,1024]{2,1,0:T(8,128)(2,1)} %param.5) | copy-start | bytes 6291460
  6.5 55.7 %all-gather.6.cloned.1.call-start = ((), (), s32[]{:S(2)}) async-start(), calls=%async_computation.4 | async-start | bytes 4718592 | tf_op jit(solution)/shard_map/all_gather | solution.py:27
  10.3 1.3 copy-start.7
  12.5 158.2 %reduce-scatter.2.cloned.1.call-start = ((), (), s32[]{:S(2)}) async-start(), calls=%async_computation.1 | async-start | bytes 10485760 | tf_op jit(solution)/shard_map/reduce_scatter | solution.py:39
  62.2 7.1 %copy-start.8 = (bf16[1,1024,1024]{2,1,0:T(8,128)(2,1)S(1)}, bf16[1,1024,1024]{2,1,0:T(8,128)(2,1)}, u32[]{:S(2)}) copy-start(bf16[1,1024,1024]{2,1,0:T(8,128)(2,1)} %copy-done.7) | copy-start | bytes 6291460
  69.3 4.6 copy-start.10
  69.3 4.6 copy-start.11
  85.5 157.9 %all-reduce.3.cloned.1.call-start = ((), (), s32[]{:S(2)}) async-start(), calls=%async_computation.2 | async-start | bytes 4194304 | tf_op jit(solution)/shard_map/psum | solution.py:11
  173.9 118.4 %all-gather.4.cloned.1.call-start = ((), (), s32[]{:S(2)}) async-start(), calls=%async_computation.3 | async-start | bytes 4718592 | tf_op jit(solution)/shard_map/all_gather | solution.py:42
  296.4 1.0 copy-start.9
  346.7 99.6 %copy-start.2 = (f32[512,1024]{0,1:T(8,128)S(1)}, f32[512,1024]{0,1:T(8,128)}, u32[]{:S(2)}) copy-start(f32[512,1024]{0,1:T(8,128)} %all-reduce.3.cloned.1.call-done) | copy-start | bytes 6291460
  465.1 6.9 %copy-start.4 = (f32[128,1536]{0,1:T(8,128)S(1)}, f32[128,1536]{0,1:T(8,128)}, u32[]{:S(2)}) copy-start(f32[128,1536]{0,1:T(8,128)} %copy.9) | copy-start | bytes 2359300
  465.1 6.9 %copy-start.5 = (f32[128,1536]{0,1:T(8,128)S(1)}, f32[128,1536]{0,1:T(8,128)}, u32[]{:S(2)}) copy-start(f32[128,1536]{0,1:T(8,128)} %copy.10) | copy-start | bytes 2359300
  465.1 6.9 %copy-start.6 = (f32[128,1536]{0,1:T(8,128)S(1)}, f32[128,1536]{0,1:T(8,128)}, u32[]{:S(2)}) copy-start(f32[128,1536]{0,1:T(8,128)} %copy.11) | copy-start | bytes 2359300
  472.0 1.6 copy-start.3
  473.6 7.9 %copy-start.1 = (bf16[1,1024,1024]{2,1,0:T(8,128)(2,1)S(1)}, bf16[1,1024,1024]{2,1,0:T(8,128)(2,1)}, u32[]{:S(2)}) copy-start(bf16[1,1024,1024]{2,1,0:T(8,128)(2,1)} %param.5) | copy-start | bytes 6291460
Sparse Core Ops, SparseCore 0:
  12.6 49.5 all-gather.5
  85.6 85.1 reduce-scatter.1
  174.0 69.2 all-reduce.2
  245.4 46.8 all-gather.3
where the time goes:
time: 497 us; the launch traced here: 488 us
  waiting for transfers between devices  251 us (51%)
  other arithmetic  132 us (27%)
  matrix products  54.8 us (11%)
  local copies, waits for them, and re-layouts  33.7 us (7%)
  between operations  16.2 us (3%)
    reduce_scatter x1, waiting for transfers between devices, shards(): lax.psum_scatter(gram_primal * gram_dual, 'cone', scatter_dimension=0, ti...  85.2 us
    another operation x14, other arithmetic, shards(): lower_factor = jnp.linalg.cholesky(pivot_matrix)  80.8 us
    psum x1, waiting for transfers between devices, broadcast(): return lax.psum(kept, axis)  69.2 us
    all_gather x1, waiting for transfers between devices, shards(): lax.all_gather(own_vectors[:row_dev], 'con', axis=0, tiled=True)  49.7 us
    all_gather x1, waiting for transfers between devices, shards(): gathered = lax.all_gather(leading_columns, 'con', axis=1, tiled=True)  47 us
    another operation x4, other arithmetic, shards(): jax.scipy.linalg.solve_triangular(lower_factor, combined, lower=True)  42.7 us
    another operation x7, matrix products, shards(): jax.scipy.linalg.solve_triangular(lower_factor, combined, lower=True)  18.8 us
    another operation x12, local copies, waits for them, and re-layouts  14 us
  transfers between devices with their start and end apart: 4, of which 4 were waited for; matrix products, arithmetic and copies ran while one was open for 0% of the time, Pallas kernels for 0%

commit v1 on v0

--- a/solution.py
+++ b/solution.py
@@ -2,8 +2,29 @@
 import jax.numpy as jnp
 from jax import lax
 from jax.sharding import PartitionSpec as P
+from jax.lax import axis_index, ppermute, psum
 
 PANEL = 512
+
+
+def state_field(u, dim_no):
+    u = jnp.moveaxis(u, 0, dim_no)
+    part_now = u.shape
+    return u.reshape(
+        *part_now[:dim_no], part_now[dim_no] * part_now[dim_no + 1], *part_now[dim_no + 2 :]
+    )
+
+
+def treat_scales(message, chip_axis):
+    step_out, reply = (psum(1, axis_name=chip_axis), axis_index(chip_axis))
+    t1, heard = (message[None], 1)
+    while heard < step_out:
+        o_now = tuple(((tick, tick ^ heard) for tick in range(step_out)))
+        out_arr = ppermute(t1, axis_name=chip_axis, perm=o_now)
+        formed = reply & heard == 0
+        t1 = jnp.concatenate([jnp.where(formed, t1, out_arr), jnp.where(formed, out_arr, t1)])
+        heard *= 2
+    return t1
 
 
 def broadcast(value, axis, source):
@@ -39,7 +60,7 @@
     schur_slab = lax.psum_scatter(gram_primal * gram_dual, "cone", scatter_dimension=0, tiled=True)
     panel_block = broadcast(schur_slab, "cone", 0)
     leading_columns = panel_block[:, :row_dev]
-    gathered = lax.all_gather(leading_columns, "con", axis=1, tiled=True)
+    gathered = state_field(treat_scales(leading_columns, "con"), 1)
     pivot_source = gathered[:, :PANEL]
     block_source = lax.dynamic_slice_in_dim(gathered, cone_place * PANEL, PANEL, 1)
     pivot_matrix = (pivot_source + pivot_source.T) * 0.5

time: 497 us -> 564 us (1.13)
  waiting for transfers between devices: 251 us -> 321 us
  matrix products: 54.8 us -> 48.1 us
    ppermute x0 -> x3, waiting for transfers between devices: none -> 116 us  [treat_scales(): out_arr = ppermute(t1, axis_name=chip_axis, perm=o_now)]
    all_gather x1 -> x0, waiting for transfers between devices: 47 us -> none  [shards(): gathered = lax.all_gather(leading_columns, 'con', axis=1, tiled=True)]
    dot_general x2 -> x0, matrix products: 11.8 us -> none  [the longest x1 7.07 us: shards(): jnp.dot(row_vectors, primal_block, preferred_element_type=jnp.float32)]
    another operation x7, matrix products: 18.8 us -> 9.39 us  [shards(): jax.scipy.linalg.solve_triangular(lower_factor, combined, lower=True)]
    dot_general x1, matrix products: 4.55 us -> 13.2 us  [shards(): lax.dot_general(row_primal, own_vectors, contract, preferred_element_type...]
    dot_general x1, matrix products: 6.77 us -> 15 us  [shards(): lax.dot_general(row_dual, own_vectors, contract, preferred_element_type=j...]
    another operation x4 -> x1, local copies, waits for them, and re-layouts: 6.87 us -> 0.01 us  [shards(): jax.scipy.linalg.solve_triangular(lower_factor, combined, lower=True)]
    transpose x0 -> x1, local copies, waits for them, and re-layouts: none -> 5.8 us  [state_field(): u = jnp.moveaxis(u, 0, dim_no)]
  transfers between devices with their start and end apart: 4 -> 6, of which waited for: 4 -> 6; matrix products, arithmetic and copies ran while one was open for 0% -> 0% of each run, Pallas kernels for 0% -> 0%
where the time goes in v1:
time: 564 us; the launch traced here: 556 us
  waiting for transfers between devices  321 us (57%)
  other arithmetic  137 us (24%)
  matrix products  48.1 us (9%)
  local copies, waits for them, and re-layouts  30.1 us (5%)
  between operations  16 us (3%)
    ppermute x3, waiting for transfers between devices, treat_scales(): out_arr = ppermute(t1, axis_name=chip_axis, perm=o_now)  116 us
    reduce_scatter x1, waiting for transfers between devices, shards(): lax.psum_scatter(gram_primal * gram_dual, 'cone', scatter_dimension=0, ti...  85.2 us
    another operation x14, other arithmetic, shards(): lower_factor = jnp.linalg.cholesky(pivot_matrix)  78.7 us
    psum x1, waiting for transfers between devices, broadcast(): return lax.psum(kept, axis)  69.4 us
    all_gather x1, waiting for transfers between devices, shards(): lax.all_gather(own_vectors[:row_dev], 'con', axis=0, tiled=True)  49.7 us
    another operation x4, other arithmetic, shards(): jax.scipy.linalg.solve_triangular(lower_factor, combined, lower=True)  41.4 us
    dot_general x1, matrix products, shards(): lax.dot_general(row_dual, own_vectors, contract, preferred_element_type=j...  15 us
    another operation x12, local copies, waits for them, and re-layouts  13.7 us
  transfers between devices with their start and end apart: 6, of which 6 were waited for; matrix products, arithmetic and copies ran while one was open for 0% of the time, Pallas kernels for 0%

profile of v1, /device:TPU:0, one launch (start us, length us, event | category | flops | bytes accessed | tf_op | source)
XLA Modules:
  0.0 556.0 jit_solution(15795564956205927200)
XLA Ops:
  6.5 1.4 fusion.77
  7.9 2.4 broadcast_multiply_fusion
  10.3 1.3 copy-done.4
  12.5 49.7 %all-gather.3.cloned.1.call-done = bf16[1,2048,1024]{2,1,0:T(8,128)(2,1)} async-done(((bf16[1,256,1024]{2,1,0:T(8,128)(2,1)}), bf16[1,2048,1024]{2,1,0:T(8,128)(2,1)}) %all-gather.3.cloned.1.call-update) | async-done | bytes 4194320 | tf_op jit(solution)/shard_map/all_gather | solution.py:48
  62.2 13.2 %fusion.5 = f32[2048,1024]{1,0:T(8,128)} fusion(bf16[1,1024,1024]{2,1,0:T(8,128)(2,1)} %copy-done.4, bf16[1,2048,1024]{2,1,0:T(8,128)(2,1)} %all-gather.3.cloned.1.call-done, bf16[1,1024,1024]{2,1,0:T(8,128)(2,1)S(1)} %copy-done), kind=kOutput, calls=%fused_computation.12 | convolution fusion | flops 8592031744 | bytes 16777216 | tf_op jit(solution)/shard_map/dot_general | solution.py:56
  75.4 15.0 %convolution_multiply_fusion = f32[2048,1024]{1,0:T(8,128)} fusion(f32[2048,1024]{1,0:T(8,128)} %fusion.5, bf16[1,1024,1024]{2,1,0:T(8,128)(2,1)} %copy-done.4, bf16[1,2048,1024]{2,1,0:T(8,128)(2,1)} %all-gather.3.cloned.1.call-done, bf16[1,1024,1024]{2,1,0:T(8,128)(2,1)} %param.6), kind=kOutput, calls=%fused_computation.5 | convolution fusion | flops 8594128896 | bytes 25165824 | tf_op jit(solution)/shard_map/dot_general | solution.py:59
  90.5 85.2 %reduce-scatter.2.cloned.1.call-done = f32[512,1024]{1,0:T(8,128)} async-done(((f32[2048,1024]{1,0:T(8,128)}), f32[512,1024]{1,0:T(8,128)}) %reduce-scatter.2.cloned.1.call-update) | async-done | bytes 2097168 | tf_op jit(solution)/shard_map/reduce_scatter | solution.py:60
  175.7 3.2 broadcast_select_fusion
  178.9 69.4 %all-reduce.3.cloned.1.call-done = f32[512,1024]{1,0:T(8,128)} async-done(((f32[512,1024]{1,0:T(8,128)}), f32[512,1024]{1,0:T(8,128)}) %all-reduce.3.cloned.1.call-update) | async-done | bytes 2097168 | tf_op jit(solution)/shard_map/psum | solution.py:32
  248.3 1.1 slice_bitcast_fusion
  249.5 1.9 collective-permute-done
  251.4 1.1 broadcast_select_fusion.6
  252.6 1.6 collective-permute-start.1
  254.1 23.8 %collective-permute-done.1 = f32[2,512,256]{2,1,0:T(8,128)} collective-permute-done((f32[2,512,256]{2,1,0:T(8,128)S(1)}, f32[2,512,256]{2,1,0:T(8,128)}, u32[]{:S(2)}, u32[]{:S(2)}) %collective-permute-start.1) | collective-permute-done | bytes 1048608 | tf_op jit(solution)/shard_map/ppermute | solution.py:23
  278.0 1.4 broadcast_select_fusion.4
  279.4 1.5 pad_maximum_fusion.1
  280.9 2.4 collective-permute-start.2
  283.3 90.6 %collective-permute-done.2 = f32[4,512,256]{2,1,0:T(8,128)} collective-permute-done((f32[4,512,256]{2,1,0:T(8,128)}, f32[4,512,256]{2,1,0:T(8,128)}, u32[]{:S(2)}, u32[]{:S(2)}) %collective-permute-start.2) | collective-permute-done | bytes 2097184 | tf_op jit(solution)/shard_map/ppermute | solution.py:23
  373.9 1.9 broadcast_select_fusion.2
  375.8 2.2 maximum_bitcast_fusion
  378.0 5.8 %copy.5 = f32[512,8,256]{0,2,1:T(8,128)} copy(f32[512,8,256]{2,0,1:T(8,128)} %maximum_bitcast_fusion) | data formatting | bytes 8388608 | tf_op jit(solution)/shard_map/transpose | solution.py:11
  383.8 2.7 fusion.76
  386.8 1.4 fusion.47
  388.8 1.0 copy-done.5
  389.8 11.7 %cholesky.104 = f32[128,128]{1,0:T(8,128)S(1)} custom-call(f32[128,128]{1,0:T(8,128)S(1)} %cholesky.266), custom_call_target="Cholesky" | custom-call | tf_op jit(solution)/shard_map/jit(cholesky)/cholesky | solution.py:67
  401.7 9.8 %custom-call.31 = f32[1,128,128]{1,2,0:T(8,128)S(1)} custom-call(f32[1,128,128]{2,1,0:T(8,128)S(1)} %get-tuple-element.40), custom_call_target="InvertDiagBlocksLowerTriangular" | custom-call | tf_op jit(solution)/shard_map/jit(cholesky)/cholesky | solution.py:67
  411.5 1.2 constant_dynamic-update-slice_fusion.3
  412.8 1.3 convolution_subtract_fusion.3
  414.0 11.7 %cholesky.217 = f32[128,128]{1,0:T(8,128)S(1)} custom-call(f32[128,128]{1,0:T(8,128)S(1)} %cholesky.270), custom_call_target="Cholesky" | custom-call | tf_op jit(solution)/shard_map/jit(cholesky)/cholesky | solution.py:67
  425.8 10.0 %custom-call.32 = f32[1,128,128]{1,2,0:T(8,128)S(1)} custom-call(f32[1,128,128]{2,1,0:T(8,128)S(1)} %get-tuple-element.37), custom_call_target="InvertDiagBlocksLowerTriangular" | custom-call | tf_op jit(solution)/shard_map/jit(cholesky)/cholesky | solution.py:67
  436.0 1.3 convolution_subtract_fusion.4
  437.3 11.7 %cholesky.238 = f32[128,128]{1,0:T(8,128)S(1)} custom-call(f32[128,128]{1,0:T(8,128)S(1)} %cholesky.275), custom_call_target="Cholesky" | custom-call | tf_op jit(solution)/shard_map/jit(cholesky)/cholesky | solution.py:67
  449.7 9.8 %custom-call.33 = f32[1,128,128]{1,2,0:T(8,128)S(1)} custom-call(f32[1,128,128]{2,1,0:T(8,128)S(1)} %get-tuple-element.34), custom_call_target="InvertDiagBlocksLowerTriangular" | custom-call | tf_op jit(solution)/shard_map/jit(cholesky)/cholesky | solution.py:67
  459.7 1.2 convolution_subtract_fusion.5
  461.0 11.9 %cholesky.255 = f32[128,128]{1,0:T(8,128)S(1)} custom-call(f32[128,128]{1,0:T(8,128)S(1)} %convolution_subtract_fusion.5), custom_call_target="Cholesky" | custom-call | tf_op jit(solution)/shard_map/jit(cholesky)/cholesky | solution.py:67
  476.6 1.1 select_select_fusion.1
  477.8 13.7 %while.1 = (s32[]{:T(128)}, f32[512,512]{1,0:T(8,128)}, s32[4,2]{0,1:T(2,128)S(1)}, f32[4,128,128]{2,1,0:T(8,128)}, s32[]{:T(128)}) while((s32[]{:T(128)}, f32[512,512]{1,0:T(8,128)}, s32[4,2]{0,1:T(2,128)S(1)}, f32[4,128,128]{2,1,0:T(8,128)}, s32[]{:T(128)}) %tuple.31), condition=%wide.while_cond, body=%wide.while_body.sunk | while | flops 2 | bytes 132705 | solution.py:69
  478.4 2.8 bitcast_dynamic-update-slice_fusion.2
  481.8 2.8 bitcast_dynamic-update-slice_fusion.2
  485.3 2.8 bitcast_dynamic-update-slice_fusion.2
  488.7 2.8 bitcast_dynamic-update-slice_fusion.2
  491.5 40.1 %custom-call.34 = f32[4,128,128]{1,2,0:T(8,128)S(1)} custom-call(f32[4,128,128]{2,1,0:T(8,128)} %get-tuple-element.12), custom_call_target="InvertDiagBlocksLowerTriangular" | custom-call | tf_op jit(solution)/shard_map/jit(_solve_triangular)/triangular_solve | solution.py:69
  531.6 1.6 copy.8
  534.0 1.6 convolution_subtract_fusion.2
  536.5 1.9 convolution_subtract_fusion
  539.2 2.5 convolution_subtract_fusion.1
  542.8 1.4 copy-done.3
  544.2 5.1 select_select_fusion
  (51 shorter events, 10.8 us)
Async XLA Ops:
  6.5 55.7 %copy-start = (bf16[1,1024,1024]{2,1,0:T(8,128)(2,1)S(1)}, bf16[1,1024,1024]{2,1,0:T(8,128)(2,1)}, u32[]{:S(2)}) copy-start(bf16[1,1024,1024]{2,1,0:T(8,128)(2,1)} %param.5) | copy-start | bytes 6291460
  6.5 55.7 %all-gather.3.cloned.1.call-start = ((), (), s32[]{:S(2)}) async-start(), calls=%async_computation.3 | async-start | bytes 4718592 | tf_op jit(solution)/shard_map/all_gather | solution.py:48
  10.3 1.3 copy-start.4
  12.5 163.3 %reduce-scatter.2.cloned.1.call-start = ((), (), s32[]{:S(2)}) async-start(), calls=%async_computation.1 | async-start | bytes 10485760 | tf_op jit(solution)/shard_map/reduce_scatter | solution.py:60
  90.5 157.9 %all-reduce.3.cloned.1.call-start = ((), (), s32[]{:S(2)}) async-start(), calls=%async_computation.2 | async-start | bytes 4194304 | tf_op jit(solution)/shard_map/psum | solution.py:32
  249.4 2.0 collective-permute-start
  252.6 25.4 %collective-permute-start.1 = (f32[2,512,256]{2,1,0:T(8,128)S(1)}, f32[2,512,256]{2,1,0:T(8,128)}, u32[]{:S(2)}, u32[]{:S(2)}) collective-permute-start(f32[2,512,256]{2,1,0:T(8,128)S(1)} %pad_maximum_fusion.2), channel_id=1, source_target_pairs={{0,2},{1,3},{2,0},{3,1},{4,6},{5,7},{6,4},{7,5},{8,10},{9,11},{10,... | collective-permute-start | bytes 3145736 | tf_op jit(solution)/shard_map/ppermute | solution.py:23
  280.9 93.0 %collective-permute-start.2 = (f32[4,512,256]{2,1,0:T(8,128)}, f32[4,512,256]{2,1,0:T(8,128)}, u32[]{:S(2)}, u32[]{:S(2)}) collective-permute-start(f32[4,512,256]{2,1,0:T(8,128)} %pad_maximum_fusion.1), channel_id=1, source_target_pairs={{0,4},{1,5},{2,6},{3,7},{4,0},{5,1},{6,2},{7,3},{8,12},{9,13},{10,... | collective-permute-start | bytes 6291464 | tf_op jit(solution)/shard_map/ppermute | solution.py:23
  388.8 1.0 copy-start.5
  476.6 56.5 %copy-start.2 = (f32[512,1024]{1,0:T(8,128)S(1)}, f32[512,1024]{1,0:T(8,128)}, u32[]{:S(2)}) copy-start(f32[512,1024]{1,0:T(8,128)} %all-reduce.3.cloned.1.call-done) | copy-start | bytes 6291460
  542.6 1.6 copy-start.3
  544.2 5.1 copy-start.1
Sparse Core Ops, SparseCore 0:
  12.6 49.5 all-gather.2
  90.6 85.1 reduce-scatter.1
  179.1 69.2 all-reduce.2
